TPU v7x, 32 devices: a whole 2x2x4 slice. The times are simulated.
32 devices in a mesh: lat: 8 (over z, x), ch: 4 (over y, core).
Axes of the slice: x: 2, y: 2, z: 4, core: 2. Of those that a mesh axis runs over, the one named last changes fastest.
Arguments:
- tokens: bfloat16 [1, 16, 8, 69120], P(None, 'lat', 'ch'), may hold values from -6 to 6
- cotangent: bfloat16 [1, 16, 8, 69120], P(None, 'lat', 'ch'), may hold values from -6 to 6
- first_weight: bfloat16 [2, 8, 96, 96], P(None, 'ch'), may hold values from -0.4375 to 0.4375
- first_bias: bfloat16 [2, 8, 96], P(None, 'ch'), may hold values from -6 to 6
- second_weight: bfloat16 [2, 8, 96, 96], P(None, 'ch'), may hold values from -0.4375 to 0.4375
- relu_mask: int32 [1, 2, 8, 256, 1536], P(None, None, 'ch', 'lat'), may hold values 0 or 1
- shrink_mask: int32 [1, 2, 8, 256, 1536], P(None, None, 'ch', 'lat'), may hold values 0 or 1
Outputs:
- token_gradient: bfloat16 [1, 16, 8, 69120], P(None, 'lat', 'ch')
- first_gradient: float32 [2, 8, 96, 96], P(None, 'ch')
- bias_gradient: float32 [2, 8, 96], P(None, 'ch')
- second_gradient: float32 [2, 8, 96, 96], P(None, 'ch')
All inputs are finite; a program needn't handle non-finite values. No bound on the sum of `relu_mask` or of `shrink_mask` on one device may be relied on, other than what follows from the above.
Results may differ from a plain program's by a relative error of at most 0.0093.
Values may be sent and summed in bfloat16 or wider, within the bound.
No kernel may reach another device: no remote copies, remote signals or barrier semaphores. Data moves between devices by JAX's collectives and lax.ppermute only.
A program may use at most 64 MiB of HBM per device.

v0:
```python
import math
import jax
import jax.numpy as jnp
from jax import lax
from jax.sharding import PartitionSpec as P

WAVES = 256


def east_basis(count, waves):
    column = jnp.arange(count, dtype=jnp.int32)[:, None]
    number = jnp.arange(waves, dtype=jnp.int32)[None, :]
    phase = (column * number % count).astype(jnp.float32) * (2.0 * math.pi / count)
    factor = 1.0 / math.sqrt(count)
    return jnp.stack([jnp.cos(phase) * factor, -jnp.sin(phase) * factor], axis=1)


def north_basis(count):
    column = jnp.arange(count, dtype=jnp.int32)[:, None]
    number = jnp.arange(count, dtype=jnp.int32)[None, :]
    phase = (column * number % count).astype(jnp.float32) * (2.0 * math.pi / count)
    factor = 1.0 / math.sqrt(count)
    cosine = jnp.cos(phase) * factor
    sine = jnp.sin(phase) * factor
    upper = jnp.concatenate([cosine, sine], axis=1)
    lower = jnp.concatenate([-sine, cosine], axis=1)
    return jnp.concatenate([upper, lower], axis=0)


def complex_mix(left_real, left_imag, right_real, right_imag, form):
    real_part = jnp.einsum(
        form, left_real, right_real, preferred_element_type=jnp.float32
    ) - jnp.einsum(form, left_imag, right_imag, preferred_element_type=jnp.float32)
    imag_part = jnp.einsum(
        form, left_real, right_imag, preferred_element_type=jnp.float32
    ) + jnp.einsum(form, left_imag, right_real, preferred_element_type=jnp.float32)
    return (real_part, imag_part)


def local(tokens, cotangent, first_weight, first_bias, second_weight, relu_mask, shrink_mask):
    batches, lat_rows, blocks_dev, flat_east = tokens.shape
    block_width = first_weight.shape[2]
    east_cells = flat_east // block_width
    east_table = east_basis(east_cells, WAVES).astype(jnp.bfloat16)

    def to_waves(field):
        grid = field.reshape(batches, lat_rows, blocks_dev, east_cells, block_width)
        return jnp.einsum(
            "bhnwe,wsk->bsnkhe", grid, east_table, preferred_element_type=jnp.float32
        ).astype(jnp.bfloat16)

    spec_tokens = lax.all_to_all(to_waves(tokens), "lat", split_axis=3, concat_axis=4, tiled=True)
    spec_cotangent = lax.all_to_all(
        to_waves(cotangent), "lat", split_axis=3, concat_axis=4, tiled=True
    )
    wave_dev = spec_tokens.shape[3]
    north_cells = spec_tokens.shape[4]
    north_table = (
        north_basis(north_cells).astype(jnp.bfloat16).reshape(2, north_cells, 2, north_cells)
    )
    factor = 1.0 / math.sqrt(north_cells * WAVES)
    shape_modes = (batches, 2, blocks_dev, wave_dev, north_cells, block_width)

    def to_modes(spec):
        return jnp.einsum(
            "tqsp,bsnkpe->btnkqe", north_table, spec, preferred_element_type=jnp.float32
        ).astype(jnp.bfloat16)

    relu_keep = relu_mask.reshape(shape_modes).astype(jnp.float32)
    shrink_keep = shrink_mask.reshape(shape_modes).astype(jnp.bfloat16)
    modes = to_modes(spec_tokens)
    upstream = to_modes(spec_cotangent) * shrink_keep
    before_real, before_imag = complex_mix(
        modes[:, 0], modes[:, 1], first_weight[0], first_weight[1], "bnkqe,nef->bnkqf"
    )
    bias_real = first_bias[0].astype(jnp.float32)[None, :, None, None, :]
    bias_imag = first_bias[1].astype(jnp.float32)[None, :, None, None, :]
    hidden_real = (relu_keep[:, 0] * (before_real + bias_real)).astype(jnp.bfloat16)
    hidden_imag = (relu_keep[:, 1] * (before_imag + bias_imag)).astype(jnp.bfloat16)
    second_real, second_imag = complex_mix(
        hidden_real, -hidden_imag, upstream[:, 0], upstream[:, 1], "bnkqe,bnkqf->nef"
    )
    second_grad = jnp.stack([second_real, second_imag]) * factor
    back_real, back_imag = complex_mix(
        upstream[:, 0], upstream[:, 1], second_weight[0], -second_weight[1], "bnkqf,nef->bnkqe"
    )
    inner_real = (relu_keep[:, 0] * back_real).astype(jnp.bfloat16)
    inner_imag = (relu_keep[:, 1] * back_imag).astype(jnp.bfloat16)
    first_real, first_imag = complex_mix(
        modes[:, 0], -modes[:, 1], inner_real, inner_imag, "bnkqe,bnkqf->nef"
    )
    first_grad = jnp.stack([first_real, first_imag]) * factor
    bias_grad = (
        jnp.stack(
            [
                jnp.sum(inner_real.astype(jnp.float32), axis=(0, 2, 3)),
                jnp.sum(inner_imag.astype(jnp.float32), axis=(0, 2, 3)),
            ]
        )
        * factor
    )
    first_grad, bias_grad, second_grad = lax.psum((first_grad, bias_grad, second_grad), "lat")
    mode_real, mode_imag = complex_mix(
        inner_real, inner_imag, first_weight[0], -first_weight[1], "bnkqf,nef->bnkqe"
    )
    stacked = jnp.stack([mode_real, mode_imag], axis=1).astype(jnp.bfloat16)
    returned = jnp.einsum(
        "tqsp,btnkqe->bsnkpe", north_table, stacked, preferred_element_type=jnp.float32
    ).astype(jnp.bfloat16)
    returned = lax.all_to_all(returned, "lat", split_axis=4, concat_axis=3, tiled=True)
    token_grad = jnp.einsum(
        "bsnkhe,wsk->bhnwe", returned, east_table, preferred_element_type=jnp.float32
    )
    token_grad = token_grad.reshape(batches, lat_rows, blocks_dev, flat_east)
    token_gradient = (token_grad + cotangent.astype(jnp.float32)).astype(jnp.bfloat16)
    return (token_gradient, first_grad, bias_grad, second_grad)


def solution(mesh):
    return jax.shard_map(
        local,
        mesh=mesh,
        in_specs=(
            P(None, "lat", "ch", None),
            P(None, "lat", "ch", None),
            P(None, "ch", None, None),
            P(None, "ch", None),
            P(None, "ch", None, None),
            P(None, None, "ch", "lat", None),
            P(None, None, "ch", "lat", None),
        ),
        out_specs=(
            P(None, "lat", "ch", None),
            P(None, "ch", None, None),
            P(None, "ch", None),
            P(None, "ch", None, None),
        ),
        check_vma=False,
    )
```

profile of v0, /device:TPU:0, one launch (start us, length us, event | category | flops | bytes accessed | tf_op | source)
XLA Modules:
  0.0 157.0 jit_solution(12354883418392423553)
XLA Ops:
  7.2 3.3 %multiply_convert_fusion = (bf16[720,1,256]{2,0,1:T(8,128)(2,1)S(1)}, bf16[720,1,256]{2,0,1:T(8,128)(2,1)S(1)}) fusion(), kind=kLoop, calls=%fused_computation.70 | loop fusion | flops 2580480 | bytes 737280 | tf_op jit(solution)/shard_map/convert.17
  10.5 2.0 %reshape.257 = bf16[2,2,720,96]{3,2,1,0:T(8,128)(2,1)S(1)} reshape(bf16[1,2,2,69120]{3,2,1,0:T(2,128)(2,1)} %param.7) | data formatting | bytes 1105920 | tf_op jit(solution)/shard_map/reshape.34
  12.5 0.5 fusion.26
  13.0 1.2 copy.86
  14.2 7.3 %all-to-all-start.2 = ((bf16[1,2,2,256,2,96]{5,2,4,1,0,3:T(2,128)(2,1)}), bf16[1,2,2,256,2,96]{5,2,4,1,0,3:T(2,128)(2,1)}, u32[]{:S(2)}, u32[]{:S(2)}) async-start(bf16[1,2,2,256,2,96]{5,2,4,1,0,3:T(2,128)(2,1)} %copy.86), calls=%async_computation.2 | async-start | bytes 1048576 | tf_op jit(solution)/shard_map/all_to_all | solution.py:52
  21.4 0.1 negate_convert_fusion
  21.5 0.1 fusion.106
  21.6 0.1 maximum_maximum_fusion
  21.7 0.1 convert_element_type.159
  21.8 0.3 convert_element_type.154
  22.2 0.6 copy-done
  22.8 0.7 reshape.249
  23.5 1.3 fusion.25
  24.8 2.0 %copy.69 = bf16[1,2,2,256,2,96]{5,2,4,1,0,3:T(2,128)(2,1)} copy(bf16[1,2,2,256,2,96]{3,5,2,4,1,0:T(8,128)(2,1)} %fusion.25) | data formatting | bytes 786432 | tf_op jit(solution)/shard_map/convert_element_type | solution.py:50
  26.8 1.2 convert_element_type.163
  28.0 0.4 copy.73
  28.4 0.5 convert_element_type.164
  28.9 0.6 bitcast_convert_fusion.1
  29.5 0.1 fusion.114
  29.6 6.4 %all-to-all-done.2 = bf16[1,2,2,256,2,96]{5,2,4,1,0,3:T(2,128)(2,1)} async-done(((bf16[1,2,2,256,2,96]{5,2,4,1,0,3:T(2,128)(2,1)}), bf16[1,2,2,256,2,96]{5,2,4,1,0,3:T(2,128)(2,1)}, u32[]{:S(2)}, u32[]{:S(2)}) %all-to-all-start.2) | async-done | bytes 393248 | tf_op jit(solution)/shard_map/all_to_all | solution.py:52
  36.0 3.6 %all-to-all-start = ((bf16[1,2,2,256,2,96]{5,2,4,1,0,3:T(2,128)(2,1)}), bf16[1,2,2,256,2,96]{5,2,4,1,0,3:T(2,128)(2,1)S(1)}, u32[]{:S(2)}, u32[]{:S(2)}) async-start(bf16[1,2,2,256,2,96]{5,2,4,1,0,3:T(2,128)(2,1)} %copy.69), calls=%async_computation | async-start | bytes 1048576 | tf_op jit(solution)/shard_map/all_to_all | solution.py:53
  39.7 1.1 copy.87
  40.8 0.5 copy.88
  41.3 0.3 fusion.3
  41.7 1.0 fusion.53
  42.8 1.0 fusion.55
  43.8 10.5 %all-to-all-done = bf16[1,2,2,256,2,96]{5,2,4,1,0,3:T(2,128)(2,1)S(1)} async-done(((bf16[1,2,2,256,2,96]{5,2,4,1,0,3:T(2,128)(2,1)}), bf16[1,2,2,256,2,96]{5,2,4,1,0,3:T(2,128)(2,1)S(1)}, u32[]{:S(2)}, u32[]{:S(2)}) %all-to-all-start) | async-done | bytes 393248 | tf_op jit(solution)/shard_map/all_to_all | solution.py:53
  54.3 0.1 copy.70
  54.4 0.5 copy.71
  55.0 0.3 fusion.10
  55.4 0.5 copy-done.8
  55.9 0.2 fusion.69
  56.1 0.2 fusion.71
  56.4 0.3 fusion.31
  56.7 0.9 convolution_bitcast_fusion.4
  57.6 0.9 convolution_bitcast_fusion.6
  58.5 0.9 convert_reduce_fusion.1
  59.5 0.2 fusion.78
  59.7 0.2 fusion.80
  59.9 1.0 convert_reduce_fusion
  60.9 0.9 convolution_bitcast_fusion.10
  61.8 0.9 convolution_bitcast_fusion.8
  62.7 0.2 fusion.28
  62.9 0.2 fusion.27
  63.2 0.1 maximum_bitcast_fusion
  63.3 0.3 fusion.4
  63.6 1.3 copy.81
  65.0 3.7 %all-to-all-start.1 = ((bf16[1,2,2,32,16,96]{5,1,3,2,0,4:T(2,128)(2,1)}), bf16[1,2,2,32,16,96]{5,1,3,2,0,4:T(2,128)(2,1)S(1)}, u32[]{:S(2)}, u32[]{:S(2)}) async-start(bf16[1,2,2,32,16,96]{5,1,3,2,0,4:T(2,128)(2,1)} %copy.81), calls=%async_computation.1 | async-start | bytes 1048576 | tf_op jit(solution)/shard_map/all_to_all | solution.py:110
  68.7 1.4 fusion.29
  70.1 0.3 fusion.37
  70.4 0.3 fusion.39
  70.7 0.7 maximum_multiply_fusion.1
  71.4 0.3 fusion.33
  71.7 0.3 fusion.35
  72.0 0.7 maximum_multiply_fusion
  72.7 22.6 %psum.22 = f32[2,2,96]{2,1,0:T(2,128)} all-reduce(f32[2,2,96]{2,1,0:T(2,128)S(1)} %maximum_multiply_fusion.2), channel_id=1, replica_groups=mesh['lat'=8,'ch'=4] {'lat'}, use_global_device_ids=true, to_apply=%region_3.4 | all-reduce | flops 384 | bytes 3072 | tf_op jit(solution)/shard_map/psum | solution.py:102
  95.4 0.1 copy.141
  95.5 0.5 convolution_bitcast_fusion
  96.0 0.5 copy.84
  96.5 1.5 reshape.256
  97.9 1.4 add_convert_fusion
  99.3 47.6 %all-reduce.3.cloned.1.call-done = (f32[2,2,96,96]{3,2,1,0:T(8,128)}, f32[2,2,96,96]{3,2,1,0:T(8,128)}) async-done(((f32[2,2,96,96]{3,2,1,0:T(8,128)}, f32[2,2,96,96]{3,2,1,0:T(8,128)}), (f32[2,2,96,96]{3,2,1,0:T(8,128)}, f32[2,2,96,96]{3,2,1,0:T(8,128)})) %all-reduce.3.cloned.1.call-update) | async-done | bytes 294928 | tf_op jit(solution)/shard_map/psum | solution.py:102
  146.9 1.6 %copy.200 = f32[2,2,96,96]{3,2,1,0:T(8,128)} copy(f32[2,2,96,96]{3,2,1,0:T(8,128)} %get-tuple-element.23) | data formatting | bytes 294912
  148.5 1.6 %copy.201 = f32[2,2,96,96]{3,2,1,0:T(8,128)} copy(f32[2,2,96,96]{3,2,1,0:T(8,128)} %get-tuple-element.25) | data formatting | bytes 294912
  (39 shorter events, 0.3 us)
Async XLA Ops:
  10.5 13.1 %copy-start.3 = (bf16[720,1,256]{2,0,1:T(8,128)(2,1)}, bf16[720,1,256]{2,0,1:T(8,128)(2,1)S(1)}, u32[]{:S(2)}) copy-start(bf16[720,1,256]{2,0,1:T(8,128)(2,1)S(1)} %get-tuple-element.18) | copy-start | bytes 1105924
  10.5 13.1 %copy-start.5 = (bf16[720,1,256]{2,0,1:T(8,128)(2,1)}, bf16[720,1,256]{2,0,1:T(8,128)(2,1)S(1)}, u32[]{:S(2)}) copy-start(bf16[720,1,256]{2,0,1:T(8,128)(2,1)S(1)} %get-tuple-element.19) | copy-start | bytes 1105924
  13.0 8.8 %copy-start.7 = (s32[1,2,2,32,1536]{4,3,2,1,0:T(8,128)S(1)}, s32[1,2,2,32,1536]{4,3,2,1,0:T(8,128)}, u32[]{:S(2)}) copy-start(s32[1,2,2,32,1536]{4,3,2,1,0:T(8,128)} %param.12) | copy-start | bytes 2359300
  14.2 21.9 %all-to-all-start.2 = ((bf16[1,2,2,256,2,96]{5,2,4,1,0,3:T(2,128)(2,1)}), bf16[1,2,2,256,2,96]{5,2,4,1,0,3:T(2,128)(2,1)}, u32[]{:S(2)}, u32[]{:S(2)}) async-start(bf16[1,2,2,256,2,96]{5,2,4,1,0,3:T(2,128)(2,1)} %copy.86), calls=%async_computation.2 | async-start | bytes 1048576 | tf_op jit(solution)/shard_map/all_to_all | solution.py:52
  21.7 1.1 copy-start
  26.8 2.1 %copy-start.12 = (bf16[2,2,96]{2,1,0:T(2,128)(2,1)S(1)}, bf16[2,2,96]{2,1,0:T(2,128)(2,1)}, u32[]{:S(2)}) copy-start(bf16[2,2,96]{2,1,0:T(2,128)(2,1)} %param.10) | copy-start | bytes 2308
  36.0 18.3 %all-to-all-start = ((bf16[1,2,2,256,2,96]{5,2,4,1,0,3:T(2,128)(2,1)}), bf16[1,2,2,256,2,96]{5,2,4,1,0,3:T(2,128)(2,1)S(1)}, u32[]{:S(2)}, u32[]{:S(2)}) async-start(bf16[1,2,2,256,2,96]{5,2,4,1,0,3:T(2,128)(2,1)} %copy.69), calls=%async_computation | async-start | bytes 1048576 | tf_op jit(solution)/shard_map/all_to_all | solution.py:53
  40.8 1.0 copy-start.2
  55.0 0.9 copy-start.8
  55.3 1.1 copy-start.1
  55.3 1.0 copy-start.9
  65.0 30.4 %all-to-all-start.1 = ((bf16[1,2,2,32,16,96]{5,1,3,2,0,4:T(2,128)(2,1)}), bf16[1,2,2,32,16,96]{5,1,3,2,0,4:T(2,128)(2,1)S(1)}, u32[]{:S(2)}, u32[]{:S(2)}) async-start(bf16[1,2,2,32,16,96]{5,1,3,2,0,4:T(2,128)(2,1)} %copy.81), calls=%async_computation.1 | async-start | bytes 1048576 | tf_op jit(solution)/shard_map/all_to_all | solution.py:110
  68.6 78.3 %all-reduce.3.cloned.1.call-start = ((), (), s32[]{:S(2)}) async-start(), calls=%async_computation.3 | async-start | bytes 786432 | tf_op jit(solution)/shard_map/psum | solution.py:102
  68.7 1.4 copy-start.14
  68.7 1.7 %copy-start.13 = (f32[2,96,96]{2,1,0:T(8,128)S(1)}, f32[2,96,96]{2,1,0:T(8,128)}, u32[]{:S(2)}) copy-start(f32[2,96,96]{2,1,0:T(8,128)} %convolution_bitcast_fusion.4) | copy-start | bytes 221188
  68.7 2.7 %copy-start.16 = (f32[2,96,96]{2,1,0:T(8,128)S(1)}, f32[2,96,96]{2,1,0:T(8,128)}, u32[]{:S(2)}) copy-start(f32[2,96,96]{2,1,0:T(8,128)} %convolution_bitcast_fusion.10) | copy-start | bytes 221188
  70.4 1.2 copy-start.15
  71.7 1.0 copy-start.10
  71.7 1.0 copy-start.11
  71.7 23.8 %copy-start.4 = (bf16[720,1,256]{2,0,1:T(8,128)(2,1)S(1)}, bf16[720,1,256]{2,0,1:T(8,128)(2,1)}, u32[]{:S(2)}) copy-start(bf16[720,1,256]{2,0,1:T(8,128)(2,1)} %copy-done.3) | copy-start | bytes 1105924
  71.7 23.8 %copy-start.6 = (bf16[720,1,256]{2,0,1:T(8,128)(2,1)S(1)}, bf16[720,1,256]{2,0,1:T(8,128)(2,1)}, u32[]{:S(2)}) copy-start(bf16[720,1,256]{2,0,1:T(8,128)(2,1)} %copy-done.5) | copy-start | bytes 1105924
Sparse Core Ops, SparseCore 0:
  73.4 73.4 all-reduce.2
where the time goes:
time: 158 us; the launch traced here: 157 us
  waiting for transfers between devices  64.6 us (41%)
  blocking collectives  22.6 us (14%)
  local copies, waits for them, and re-layouts  17.4 us (11%)
  matrix products  15 us (9%)
  starting transfers between devices  14.6 us (9%)
  between operations  14.5 us (9%)
  other arithmetic  8.23 us (5%)
    psum x1, waiting for transfers between devices, local(): lax.psum((first_grad, bias_grad, second_grad), 'lat')  47.6 us
    psum x1, blocking collectives, local(): lax.psum((first_grad, bias_grad, second_grad), 'lat')  22.6 us
    all_to_all x1, waiting for transfers between devices, local(): lax.all_to_all(to_waves(cotangent), 'lat', split_axis=3, concat_axis=4, t...  10.5 us
    all_to_all x1, starting transfers between devices, local(): lax.all_to_all(to_waves(tokens), 'lat', split_axis=3, concat_axis=4, tile...  7.28 us
    all_to_all x1, waiting for transfers between devices, local(): lax.all_to_all(to_waves(tokens), 'lat', split_axis=3, concat_axis=4, tile...  6.44 us
    unnamed x36, local copies, waits for them, and re-layouts  4.46 us
    dot_general x5, matrix products, complex_mix(): jnp.einsum(form, left_imag, right_imag, preferred_element_type=jnp.float32)  4.39 us
    all_to_all x1, starting transfers between devices, local(): lax.all_to_all(returned, 'lat', split_axis=4, concat_axis=3, tiled=True)  3.65 us
  transfers between devices with their start and end apart: 4, of which 3 were waited for; matrix products, arithmetic and copies ran while one was open for 12% of the time, Pallas kernels for 0%

commit v1 on v0

--- a/solution.py
+++ b/solution.py
@@ -38,6 +38,26 @@
 
 
 def local(tokens, cotangent, first_weight, first_bias, second_weight, relu_mask, shrink_mask):
+
+    def handle_gates(content):
+        s_next, newest = (lax.axis_size("lat"), lax.axis_index("lat"))
+        r_now = content.shape[3] // s_next
+        mixed_arr = list(content.shape)
+        mixed_arr[3] = r_now
+        all_rows = mixed_arr[4]
+        mixed_arr[4] = all_rows * s_next
+        reply = jnp.zeros(mixed_arr, content.dtype)
+        for t in range(s_next):
+            piece_out = lax.dynamic_slice_in_dim(content, (newest ^ t) * r_now, r_now, axis=3)
+            if t:
+                piece_out = lax.ppermute(
+                    piece_out, "lat", perm=tuple(((i0, i0 ^ t) for i0 in range(s_next)))
+                )
+            reply = lax.dynamic_update_slice_in_dim(
+                reply, piece_out, (newest ^ t) * all_rows, axis=4
+            )
+        return reply
+
     batches, lat_rows, blocks_dev, flat_east = tokens.shape
     block_width = first_weight.shape[2]
     east_cells = flat_east // block_width
@@ -49,7 +69,7 @@
             "bhnwe,wsk->bsnkhe", grid, east_table, preferred_element_type=jnp.float32
         ).astype(jnp.bfloat16)
 
-    spec_tokens = lax.all_to_all(to_waves(tokens), "lat", split_axis=3, concat_axis=4, tiled=True)
+    spec_tokens = handle_gates(to_waves(tokens))
     spec_cotangent = lax.all_to_all(
         to_waves(cotangent), "lat", split_axis=3, concat_axis=4, tiled=True
     )

time: 158 us -> 156 us (0.987)
  waiting for transfers between devices: 64.6 us -> 51 us
  local copies, waits for them, and re-layouts: 17.4 us -> 28.5 us
  starting transfers between devices: 14.6 us -> 22.6 us
  matrix products: 15 us -> 9.29 us
  other arithmetic: 8.23 us -> 6.52 us
    ppermute x0 -> x7, starting transfers between devices: none -> 14.2 us  [handle_gates(): lax.ppermute(piece_out, 'lat', perm=tuple(((i0, i0 ^ t) for i0 in range(s...]
    all_to_all x1, waiting for transfers between devices: 10.5 us -> 0.01 us  [local(): lax.all_to_all(to_waves(cotangent), 'lat', split_axis=3, concat_axis=4, t...]
    another operation x3 -> x13, local copies, waits for them, and re-layouts: 2.09 us -> 9.94 us
    all_to_all x1 -> x0, starting transfers between devices: 7.28 us -> none  [local(): lax.all_to_all(to_waves(tokens), 'lat', split_axis=3, concat_axis=4, tile...]
    all_to_all x1 -> x0, waiting for transfers between devices: 6.44 us -> none  [local(): lax.all_to_all(to_waves(tokens), 'lat', split_axis=3, concat_axis=4, tile...]
    dynamic_update_slice x0 -> x8, local copies, waits for them, and re-layouts: none -> 5.11 us  [handle_gates(): lax.dynamic_update_slice_in_dim(reply, piece_out, (newest ^ t) * all_rows...]
    dot_general x5, matrix products: 4.39 us -> 2.14 us  [complex_mix(): jnp.einsum(form, left_imag, right_imag, preferred_element_type=jnp.float32)]
    convert_element_type x2 -> x1, local copies, waits for them, and re-layouts: 3.14 us -> 1.15 us  [to_waves(): return jnp.einsum('bhnwe,wsk->bsnkhe', grid, east_table, preferred_elemen...]
  transfers between devices with their start and end apart: 4 -> 10, of which waited for: 3 -> 2; matrix products, arithmetic and copies ran while one was open for 12% -> 17% of each run, Pallas kernels for 0% -> 0%
where the time goes in v1:
time: 156 us; the launch traced here: 155 us
  waiting for transfers between devices  51 us (33%)
  local copies, waits for them, and re-layouts  28.5 us (18%)
  starting transfers between devices  22.6 us (14%)
  blocking collectives  22.3 us (14%)
  between operations  14.7 us (9%)
  matrix products  9.29 us (6%)
  other arithmetic  6.52 us (4%)
    psum x1, waiting for transfers between devices, local(): lax.psum((first_grad, bias_grad, second_grad), 'lat')  49.4 us
    psum x1, blocking collectives, local(): lax.psum((first_grad, bias_grad, second_grad), 'lat')  22.3 us
    ppermute x7, starting transfers between devices, handle_gates(): lax.ppermute(piece_out, 'lat', perm=tuple(((i0, i0 ^ t) for i0 in range(s...  14.2 us
    another operation x13, local copies, waits for them, and re-layouts  9.94 us
    dynamic_update_slice x8, local copies, waits for them, and re-layouts, handle_gates(): lax.dynamic_update_slice_in_dim(reply, piece_out, (newest ^ t) * all_rows...  5.11 us
    all_to_all x1, starting transfers between devices, local(): lax.all_to_all(to_waves(cotangent), 'lat', split_axis=3, concat_axis=4, t...  4.88 us
    unnamed x30, local copies, waits for them, and re-layouts  4.55 us
    all_to_all x1, starting transfers between devices, local(): lax.all_to_all(returned, 'lat', split_axis=4, concat_axis=3, tiled=True)  3.49 us
  transfers between devices with their start and end apart: 10, of which 2 were waited for; matrix products, arithmetic and copies ran while one was open for 17% of the time, Pallas kernels for 0%

profile of v1, /device:TPU:0, one launch (start us, length us, event | category | flops | bytes accessed | tf_op | source)
XLA Modules:
  0.0 155.0 jit_solution(889561334726101264)
XLA Ops:
  7.2 3.3 %multiply_convert_fusion = (bf16[720,1,256]{2,0,1:T(8,128)(2,1)S(1)}, bf16[720,1,256]{2,0,1:T(8,128)(2,1)S(1)}) fusion(), kind=kLoop, calls=%fused_computation.69 | loop fusion | flops 2580480 | bytes 737280 | tf_op jit(solution)/shard_map/convert.17
  10.5 2.0 %reshape.310 = bf16[2,2,720,96]{3,2,1,0:T(8,128)(2,1)S(1)} reshape(bf16[1,2,2,69120]{3,2,1,0:T(2,128)(2,1)} %param.7) | data formatting | bytes 1105920 | tf_op jit(solution)/shard_map/reshape.34
  12.5 0.5 convolution_convert_fusion
  13.1 1.3 constant_dynamic-slice_fusion
  14.4 0.7 copy.101
  15.1 3.0 %collective-permute-start = (bf16[1,2,2,32,2,96]{5,3,2,4,0,1:T(8,128)(2,1)}, bf16[1,2,2,32,2,96]{5,3,2,4,0,1:T(8,128)(2,1)}, u32[]{:S(2)}, u32[]{:S(2)}) collective-permute-start(bf16[1,2,2,32,2,96]{5,3,2,4,0,1:T(8,128)(2,1)} %bitcast.70), channel_id=1, source_target_pairs={{0,4},{4,0},{8,12},{12,8},{16,20},{20,16},{24,28},{28,24},{1,5},{5... | collective-permute-start | bytes 147464 | tf_op jit(solution)/shard_map/ppermute | solution.py:53
  18.1 0.7 copy.103
  18.8 1.6 %collective-permute-start.1 = (bf16[1,2,2,32,2,96]{5,3,2,4,0,1:T(8,128)(2,1)}, bf16[1,2,2,32,2,96]{5,3,2,4,0,1:T(8,128)(2,1)}, u32[]{:S(2)}, u32[]{:S(2)}) collective-permute-start(bf16[1,2,2,32,2,96]{5,3,2,4,0,1:T(8,128)(2,1)} %bitcast.73), channel_id=1, source_target_pairs={{0,8},{4,12},{8,0},{12,4},{16,24},{20,28},{24,16},{28,20},{1,9},{5... | collective-permute-start | bytes 147464 | tf_op jit(solution)/shard_map/ppermute | solution.py:53
  20.4 0.7 copy.105
  21.1 0.7 copy.107
  21.9 3.0 %collective-permute-start.3 = (bf16[1,2,2,32,2,96]{5,3,2,4,0,1:T(8,128)(2,1)}, bf16[1,2,2,32,2,96]{5,3,2,4,0,1:T(8,128)(2,1)}, u32[]{:S(2)}, u32[]{:S(2)}) collective-permute-start(bf16[1,2,2,32,2,96]{5,3,2,4,0,1:T(8,128)(2,1)} %bitcast.79), channel_id=1, source_target_pairs={{0,16},{4,20},{8,24},{12,28},{16,0},{20,4},{24,8},{28,12},{1,17},{... | collective-permute-start | bytes 147464 | tf_op jit(solution)/shard_map/ppermute | solution.py:53
  24.9 0.7 copy.109
  25.6 1.3 collective-permute-start.4
  26.9 0.7 reshape.302
  27.6 0.5 fusion.25
  28.2 1.2 copy.82
  29.3 4.9 %all-to-all-start = ((bf16[1,2,2,256,2,96]{5,2,4,1,0,3:T(2,128)(2,1)}), bf16[1,2,2,256,2,96]{5,2,4,1,0,3:T(2,128)(2,1)S(1)}, u32[]{:S(2)}, u32[]{:S(2)}) async-start(bf16[1,2,2,256,2,96]{5,2,4,1,0,3:T(2,128)(2,1)} %copy.82), calls=%async_computation | async-start | bytes 1048576 | tf_op jit(solution)/shard_map/all_to_all | solution.py:73
  34.6 0.3 convert_element_type.150
  35.0 0.6 copy-done.13
  35.9 1.7 %copy.111 = bf16[2,32,2,2,96]{4,1,3,2,0:T(8,128)(2,1)} copy(bf16[2,32,2,2,96]{1,4,3,2,0:T(8,128)(2,1)} %get-tuple-element.13) | data formatting | bytes 98304 | tf_op jit(solution)/shard_map/dynamic-slice.14
  37.5 1.0 copy.113
  38.7 1.2 copy.86
  39.8 1.5 convert_element_type.160
  41.4 3.9 %collective-permute-start.5 = (bf16[1,2,2,32,2,96]{5,3,2,4,0,1:T(8,128)(2,1)}, bf16[1,2,2,32,2,96]{5,3,2,4,0,1:T(8,128)(2,1)S(1)}, u32[]{:S(2)}, u32[]{:S(2)}) collective-permute-start(bf16[1,2,2,32,2,96]{5,3,2,4,0,1:T(8,128)(2,1)} %bitcast.85), channel_id=1, source_target_pairs={{0,24},{4,28},{8,16},{12,20},{16,8},{20,12},{24,0},{28,4},{1,25},{... | collective-permute-start | bytes 147464 | tf_op jit(solution)/shard_map/ppermute | solution.py:53
  45.3 1.0 copy_dynamic-update-slice_fusion.6
  46.2 1.5 collective-permute-start.6
  47.8 1.0 copy_dynamic-update-slice_fusion.5
  48.7 1.0 copy_dynamic-update-slice_fusion.4
  49.7 1.0 copy_dynamic-update-slice_fusion.3
  50.7 1.0 copy_dynamic-update-slice_fusion.2
  51.8 1.6 %collective-permute-done.6 = bf16[1,2,2,32,2,96]{5,3,2,4,0,1:T(8,128)(2,1)S(1)} collective-permute-done((bf16[1,2,2,32,2,96]{5,3,2,4,0,1:T(8,128)(2,1)S(1)}, bf16[1,2,2,32,2,96]{5,3,2,4,0,1:T(8,128)(2,1)S(1)}, u32[]{:S(2)}, u32[]{:S(2)}) %collective-permute-start.6) | collective-permute-done | bytes 49184 | tf_op jit(solution)/shard_map/ppermute | solution.py:53
  53.5 0.4 fusion.3
  54.1 1.0 fusion.28
  55.3 1.0 fusion.30
  56.5 0.5 copy.84
  57.0 0.3 fusion.10
  57.4 0.5 copy-done.10
  57.9 0.2 fusion.69
  58.1 0.2 fusion.71
  58.4 0.3 convolution_bitcast_fusion.4
  58.6 0.3 convolution_bitcast_fusion.6
  58.9 0.4 convert_reduce_fusion.1
  59.8 0.4 convert_reduce_fusion
  60.3 0.3 convolution_bitcast_fusion.10
  60.6 0.3 convolution_bitcast_fusion.8
  60.9 0.2 fusion.27
  61.1 0.2 fusion.26
  61.5 0.3 fusion.4
  61.8 1.3 copy.94
  63.2 3.5 %all-to-all-start.1 = ((bf16[1,2,2,32,16,96]{5,1,3,2,0,4:T(2,128)(2,1)}), bf16[1,2,2,32,16,96]{5,1,3,2,0,4:T(2,128)(2,1)S(1)}, u32[]{:S(2)}, u32[]{:S(2)}) async-start(bf16[1,2,2,32,16,96]{5,1,3,2,0,4:T(2,128)(2,1)} %copy.94), calls=%async_computation.1 | async-start | bytes 1048576 | tf_op jit(solution)/shard_map/all_to_all | solution.py:130
  66.7 0.3 fusion.36
  67.0 0.3 fusion.38
  67.3 0.7 maximum_multiply_fusion.1
  68.0 0.3 fusion.32
  68.2 0.3 fusion.34
  68.5 0.7 maximum_multiply_fusion
  69.2 22.3 %psum.22 = f32[2,2,96]{2,1,0:T(2,128)} all-reduce(f32[2,2,96]{2,1,0:T(2,128)S(1)} %maximum_multiply_fusion.2), channel_id=1, replica_groups=mesh['lat'=8,'ch'=4] {'lat'}, use_global_device_ids=true, to_apply=%region_3.4 | all-reduce | flops 384 | bytes 3072 | tf_op jit(solution)/shard_map/psum | solution.py:122
  91.7 0.5 convolution_bitcast_fusion
  92.2 0.5 copy.97
  92.7 1.5 reshape.309
  94.1 1.4 add_convert_fusion
  95.5 49.4 %all-reduce.3.cloned.1.call-done = (f32[2,2,96,96]{3,2,1,0:T(8,128)}, f32[2,2,96,96]{3,2,1,0:T(8,128)}) async-done(((f32[2,2,96,96]{3,2,1,0:T(8,128)}, f32[2,2,96,96]{3,2,1,0:T(8,128)}), (f32[2,2,96,96]{3,2,1,0:T(8,128)}, f32[2,2,96,96]{3,2,1,0:T(8,128)})) %all-reduce.3.cloned.1.call-update) | async-done | bytes 294928 | tf_op jit(solution)/shard_map/psum | solution.py:122
  144.9 1.6 %copy.242 = f32[2,2,96,96]{3,2,1,0:T(8,128)} copy(f32[2,2,96,96]{3,2,1,0:T(8,128)} %get-tuple-element.31) | data formatting | bytes 294912
  146.5 1.6 %copy.243 = f32[2,2,96,96]{3,2,1,0:T(8,128)} copy(f32[2,2,96,96]{3,2,1,0:T(8,128)} %get-tuple-element.33) | data formatting | bytes 294912
  (60 shorter events, 2.6 us)
Async XLA Ops:
  10.5 17.1 %copy-start.4 = (bf16[720,1,256]{2,0,1:T(8,128)(2,1)}, bf16[720,1,256]{2,0,1:T(8,128)(2,1)S(1)}, u32[]{:S(2)}) copy-start(bf16[720,1,256]{2,0,1:T(8,128)(2,1)S(1)} %get-tuple-element.26) | copy-start | bytes 1105924
  10.5 17.1 %copy-start.6 = (bf16[720,1,256]{2,0,1:T(8,128)(2,1)}, bf16[720,1,256]{2,0,1:T(8,128)(2,1)S(1)}, u32[]{:S(2)}) copy-start(bf16[720,1,256]{2,0,1:T(8,128)(2,1)S(1)} %get-tuple-element.27) | copy-start | bytes 1105924
  13.1 13.8 %copy-start = (bf16[1,2,2,69120]{3,2,1,0:T(2,128)(2,1)S(1)}, bf16[1,2,2,69120]{3,2,1,0:T(2,128)(2,1)}, u32[]{:S(2)}) copy-start(bf16[1,2,2,69120]{3,2,1,0:T(2,128)(2,1)} %param.8) | copy-start | bytes 1658884
  15.1 26.2 %collective-permute-start = (bf16[1,2,2,32,2,96]{5,3,2,4,0,1:T(8,128)(2,1)}, bf16[1,2,2,32,2,96]{5,3,2,4,0,1:T(8,128)(2,1)}, u32[]{:S(2)}, u32[]{:S(2)}) collective-permute-start(bf16[1,2,2,32,2,96]{5,3,2,4,0,1:T(8,128)(2,1)} %bitcast.70), channel_id=1, source_target_pairs={{0,4},{4,0},{8,12},{12,8},{16,20},{20,16},{24,28},{28,24},{1,5},{5... | collective-permute-start | bytes 147464 | tf_op jit(solution)/shard_map/ppermute | solution.py:53
  18.8 27.4 %collective-permute-start.1 = (bf16[1,2,2,32,2,96]{5,3,2,4,0,1:T(8,128)(2,1)}, bf16[1,2,2,32,2,96]{5,3,2,4,0,1:T(8,128)(2,1)}, u32[]{:S(2)}, u32[]{:S(2)}) collective-permute-start(bf16[1,2,2,32,2,96]{5,3,2,4,0,1:T(8,128)(2,1)} %bitcast.73), channel_id=1, source_target_pairs={{0,8},{4,12},{8,0},{12,4},{16,24},{20,28},{24,16},{28,20},{1,9},{5... | collective-permute-start | bytes 147464 | tf_op jit(solution)/shard_map/ppermute | solution.py:53
  21.1 27.6 %collective-permute-start.2 = (bf16[1,2,2,32,2,96]{5,3,2,4,0,1:T(8,128)(2,1)}, bf16[1,2,2,32,2,96]{5,3,2,4,0,1:T(8,128)(2,1)}, u32[]{:S(2)}, u32[]{:S(2)}) collective-permute-start(bf16[1,2,2,32,2,96]{5,3,2,4,0,1:T(8,128)(2,1)} %bitcast.76), channel_id=1, source_target_pairs={{0,12},{4,8},{8,4},{12,0},{16,28},{20,24},{24,20},{28,16},{1,13},{... | collective-permute-start | bytes 147464 | tf_op jit(solution)/shard_map/ppermute | solution.py:53
  21.9 27.8 %collective-permute-start.3 = (bf16[1,2,2,32,2,96]{5,3,2,4,0,1:T(8,128)(2,1)}, bf16[1,2,2,32,2,96]{5,3,2,4,0,1:T(8,128)(2,1)}, u32[]{:S(2)}, u32[]{:S(2)}) collective-permute-start(bf16[1,2,2,32,2,96]{5,3,2,4,0,1:T(8,128)(2,1)} %bitcast.79), channel_id=1, source_target_pairs={{0,16},{4,20},{8,24},{12,28},{16,0},{20,4},{24,8},{28,12},{1,17},{... | collective-permute-start | bytes 147464 | tf_op jit(solution)/shard_map/ppermute | solution.py:53
  25.6 25.0 %collective-permute-start.4 = (bf16[1,2,2,32,2,96]{5,3,2,4,0,1:T(8,128)(2,1)}, bf16[1,2,2,32,2,96]{5,3,2,4,0,1:T(8,128)(2,1)}, u32[]{:S(2)}, u32[]{:S(2)}) collective-permute-start(bf16[1,2,2,32,2,96]{5,3,2,4,0,1:T(8,128)(2,1)} %bitcast.82), channel_id=1, source_target_pairs={{0,20},{4,16},{8,28},{12,24},{16,4},{20,0},{24,12},{28,8},{1,21},{... | collective-permute-start | bytes 147464 | tf_op jit(solution)/shard_map/ppermute | solution.py:53
  28.2 6.3 %copy-start.8 = (s32[1,2,2,32,1536]{4,3,2,1,0:T(8,128)S(1)}, s32[1,2,2,32,1536]{4,3,2,1,0:T(8,128)}, u32[]{:S(2)}) copy-start(s32[1,2,2,32,1536]{4,3,2,1,0:T(8,128)} %param.12) | copy-start | bytes 2359300
  29.3 27.1 %all-to-all-start = ((bf16[1,2,2,256,2,96]{5,2,4,1,0,3:T(2,128)(2,1)}), bf16[1,2,2,256,2,96]{5,2,4,1,0,3:T(2,128)(2,1)S(1)}, u32[]{:S(2)}, u32[]{:S(2)}) async-start(bf16[1,2,2,256,2,96]{5,2,4,1,0,3:T(2,128)(2,1)} %copy.82), calls=%async_computation | async-start | bytes 1048576 | tf_op jit(solution)/shard_map/all_to_all | solution.py:73
  34.9 0.7 copy-start.13
  35.6 3.0 %copy-start.9 = (s32[1,2,2,32,1536]{4,3,2,1,0:T(8,128)S(1)}, s32[1,2,2,32,1536]{4,3,2,1,0:T(8,128)}, u32[]{:S(2)}) copy-start(s32[1,2,2,32,1536]{4,3,2,1,0:T(8,128)} %param.13) | copy-start | bytes 2359300
  41.4 10.3 %collective-permute-start.5 = (bf16[1,2,2,32,2,96]{5,3,2,4,0,1:T(8,128)(2,1)}, bf16[1,2,2,32,2,96]{5,3,2,4,0,1:T(8,128)(2,1)S(1)}, u32[]{:S(2)}, u32[]{:S(2)}) collective-permute-start(bf16[1,2,2,32,2,96]{5,3,2,4,0,1:T(8,128)(2,1)} %bitcast.85), channel_id=1, source_target_pairs={{0,24},{4,28},{8,16},{12,20},{16,8},{20,12},{24,0},{28,4},{1,25},{... | collective-permute-start | bytes 147464 | tf_op jit(solution)/shard_map/ppermute | solution.py:53
  46.2 7.7 %copy-start.3 = (bf16[2,2,96,96]{3,2,1,0:T(8,128)(2,1)S(1)}, bf16[2,2,96,96]{3,2,1,0:T(8,128)(2,1)}, u32[]{:S(2)}) copy-start(bf16[2,2,96,96]{3,2,1,0:T(8,128)(2,1)} %param.9) | copy-start | bytes 221188
  46.2 7.1 %collective-permute-start.6 = (bf16[1,2,2,32,2,96]{5,3,2,4,0,1:T(8,128)(2,1)S(1)}, bf16[1,2,2,32,2,96]{5,3,2,4,0,1:T(8,128)(2,1)S(1)}, u32[]{:S(2)}, u32[]{:S(2)}) collective-permute-start(bf16[1,2,2,32,2,96]{5,3,2,4,0,1:T(8,128)(2,1)S(1)} %bitcast.377), channel_id=1, source_target_pairs={{0,28},{4,24},{8,20},{12,16},{16,12},{20,8},{24,4},{28,0},{1,29},{... | collective-permute-start | bytes 147464 | tf_op jit(solution)/shard_map/ppermute | solution.py:53
  53.8 1.3 copy-start.1
  57.0 0.9 copy-start.10
  57.4 1.0 copy-start.12
  59.3 1.0 copy-start.2
  61.5 5.3 %copy-start.11 = (bf16[2,32,16,96]{3,1,2,0:T(8,128)(2,1)S(1)}, bf16[2,32,16,96]{3,1,2,0:T(8,128)(2,1)}, u32[]{:S(2)}) copy-start(bf16[2,32,16,96]{3,1,2,0:T(8,128)(2,1)} %fusion.28) | copy-start | bytes 589828
  63.2 28.4 %all-to-all-start.1 = ((bf16[1,2,2,32,16,96]{5,1,3,2,0,4:T(2,128)(2,1)}), bf16[1,2,2,32,16,96]{5,1,3,2,0,4:T(2,128)(2,1)S(1)}, u32[]{:S(2)}, u32[]{:S(2)}) async-start(bf16[1,2,2,32,16,96]{5,1,3,2,0,4:T(2,128)(2,1)} %copy.94), calls=%async_computation.1 | async-start | bytes 1048576 | tf_op jit(solution)/shard_map/all_to_all | solution.py:130
  66.7 78.2 %all-reduce.3.cloned.1.call-start = ((), (), s32[]{:S(2)}) async-start(), calls=%async_computation.2 | async-start | bytes 786432 | tf_op jit(solution)/shard_map/psum | solution.py:122
  68.2 23.4 %copy-start.5 = (bf16[720,1,256]{2,0,1:T(8,128)(2,1)S(1)}, bf16[720,1,256]{2,0,1:T(8,128)(2,1)}, u32[]{:S(2)}) copy-start(bf16[720,1,256]{2,0,1:T(8,128)(2,1)} %copy-done.4) | copy-start | bytes 1105924
  68.5 23.2 %copy-start.7 = (bf16[720,1,256]{2,0,1:T(8,128)(2,1)S(1)}, bf16[720,1,256]{2,0,1:T(8,128)(2,1)}, u32[]{:S(2)}) copy-start(bf16[720,1,256]{2,0,1:T(8,128)(2,1)} %copy-done.6) | copy-start | bytes 1105924
Sparse Core Ops, SparseCore 0:
  71.5 73.3 all-reduce.2
